TPU v7x, 256 devices: a whole 4x4x8 slice. The times are simulated.
256 devices in a mesh: grp: 8 (over y, core), row: 32 (over z, x).
Axes of the slice: x: 4, y: 4, z: 8, core: 2. Of those that a mesh axis runs over, the one named last changes fastest.
Arguments:
- features: bfloat16 [524288, 256], P(('grp', 'row')), may hold values from -6 to 6
- cotangent: bfloat16 [524288, 256], P(('grp', 'row')), may hold values from -6 to 6
- self_weight: bfloat16 [256, 256], replicated, may hold values from -0.375 to 0.375
- neighbor_weight: bfloat16 [256, 256], replicated, may hold values from -0.375 to 0.375
- tile_values: bfloat16 [256, 64, 128, 128], P(('grp', 'row')), may hold values from 0 to 1
- tile_index: int32 [256, 64, 2], P(('grp', 'row')), may hold values from 0 to 15
- hub_adjacency: bfloat16 [524288, 1024], P(('grp', 'row')), may hold values from 0 to 1
- hub_owner: int32 [8, 8], P('grp'), may hold values from 0 to 31
- send_rows: int32 [256, 8, 64], P(('grp', 'row')), may hold values from 0 to 2047
- cut_adjacency: bfloat16 [524288, 512], P(('grp', 'row')), may hold values from 0 to 1
- degrees: int32 [524288], P(('grp', 'row')), may hold values from 1024 to 2047
Outputs:
- hidden: bfloat16 [524288, 256], P(('grp', 'row'))
- grad_features: bfloat16 [524288, 256], P(('grp', 'row'))
- grad_self: float32 [256, 256], replicated
- grad_neighbor: float32 [256, 256], replicated
Inputs may be any that keep to these rules, and one draw needn't show every extreme that they name: `send_rows`: rows may repeat.
All inputs are finite; a program needn't handle non-finite values.
Results may differ from a plain program's by a relative error of at most 0.014.
Values may be sent and summed in bfloat16 or wider, within the bound.
A program may use at most 128 MiB of HBM per device.

v0:
```python
import jax
import jax.numpy as jnp
from jax import lax
from jax.sharding import PartitionSpec as P

TILE = 128
HUB = 128


def spread(value, axis, root):
    mine = lax.axis_index(axis) == root
    return lax.psum(jnp.where(mine, value, jnp.zeros_like(value)), axis)


def on_device(
    features,
    cotangent,
    self_weight,
    neighbor_weight,
    tile_values,
    tile_index,
    hub_adjacency,
    hub_owner,
    send_rows,
    cut_adjacency,
    degrees,
):
    node_count, width = features.shape
    tile_total = node_count // TILE
    group_count = lax.axis_size("grp")
    section_count = hub_owner.shape[1]
    values = tile_values[0]
    index = tile_index[0]
    owners = hub_owner[0]
    blocks = features.reshape(tile_total, TILE, width)
    row_select = (index[:, 0][None, :] == jnp.arange(tile_total)[:, None]).astype(jnp.float32)
    col_select = (index[:, 1][None, :] == jnp.arange(tile_total)[:, None]).astype(jnp.float32)
    picked = blocks[index[:, 1]]
    product = jnp.einsum("lab,lbf->laf", values, picked, preferred_element_type=jnp.float32)
    local_sum = jnp.einsum(
        "nl,laf->naf", row_select, product, precision=lax.Precision.HIGHEST
    ).reshape(node_count, width)
    heads = features[:HUB]
    hub_sum = jnp.zeros((node_count, width), jnp.float32)
    for section in range(section_count):
        panel = spread(heads, "row", owners[section])
        hub_sum = hub_sum + jnp.dot(
            hub_adjacency[:, section * HUB : (section + 1) * HUB],
            panel,
            preferred_element_type=jnp.float32,
        )
    outgoing = features[send_rows[0]]
    arrived = lax.all_to_all(outgoing, "grp", split_axis=0, concat_axis=0, tiled=True)
    cut_sum = jnp.dot(
        cut_adjacency,
        arrived.reshape(group_count * outgoing.shape[1], width),
        preferred_element_type=jnp.float32,
    )
    scaling = lax.rsqrt(degrees.astype(jnp.float32))[:, None]
    aggregated = ((local_sum + hub_sum + cut_sum) * scaling).astype(jnp.bfloat16)
    before = jnp.dot(features, self_weight, preferred_element_type=jnp.float32) + jnp.dot(
        aggregated, neighbor_weight, preferred_element_type=jnp.float32
    )
    activated, pullback = jax.vjp(jax.nn.gelu, before)
    hidden = activated.astype(jnp.bfloat16)
    grad_before = pullback(cotangent.astype(jnp.float32))[0].astype(jnp.bfloat16)
    rows_dims = (((0,), (0,)), ((), ()))
    cols_dims = (((1,), (1,)), ((), ()))
    self_part = lax.dot_general(
        features, grad_before, rows_dims, preferred_element_type=jnp.float32
    )
    neighbor_part = lax.dot_general(
        aggregated, grad_before, rows_dims, preferred_element_type=jnp.float32
    )
    grad_self, grad_neighbor = lax.psum((self_part, neighbor_part), ("grp", "row"))
    grad_aggregate = (
        lax.dot_general(grad_before, neighbor_weight, cols_dims, preferred_element_type=jnp.float32)
        * scaling
    ).astype(jnp.bfloat16)
    grad_total = lax.dot_general(
        grad_before, self_weight, cols_dims, preferred_element_type=jnp.float32
    )
    agg_blocks = grad_aggregate.reshape(tile_total, TILE, width)[index[:, 0]]
    returned = jnp.einsum("lab,laf->lbf", values, agg_blocks, preferred_element_type=jnp.float32)
    grad_total = grad_total + jnp.einsum(
        "nl,lbf->nbf", col_select, returned, precision=lax.Precision.HIGHEST
    ).reshape(node_count, width)
    hub_terms = lax.dot_general(
        hub_adjacency, grad_aggregate, rows_dims, preferred_element_type=jnp.float32
    ).reshape(section_count, HUB, width)
    totals = lax.psum(hub_terms.astype(jnp.bfloat16), "row").astype(jnp.float32)
    owned = (owners == lax.axis_index("row")).astype(jnp.float32)
    hub_grad = jnp.einsum("s,shf->hf", owned, totals, precision=lax.Precision.HIGHEST)
    grad_total = grad_total.at[:HUB].add(hub_grad)
    back_rows = lax.dot_general(
        cut_adjacency, grad_aggregate, rows_dims, preferred_element_type=jnp.float32
    ).astype(jnp.bfloat16)
    back_rows = back_rows.reshape(group_count, -1, width)
    returned_rows = lax.all_to_all(back_rows, "grp", split_axis=0, concat_axis=0, tiled=True)
    scatter_table = (send_rows[0].reshape(-1)[None, :] == jnp.arange(node_count)[:, None]).astype(
        jnp.bfloat16
    )
    grad_total = grad_total + jnp.dot(
        scatter_table, returned_rows.reshape(-1, width), preferred_element_type=jnp.float32
    )
    return (hidden, grad_total.astype(jnp.bfloat16), grad_self, grad_neighbor)


def solution(mesh):
    in_specs = (
        P(("grp", "row"), None),
        P(("grp", "row"), None),
        P(),
        P(),
        P(("grp", "row"), None, None, None),
        P(("grp", "row"), None, None),
        P(("grp", "row"), None),
        P("grp", None),
        P(("grp", "row"), None, None),
        P(("grp", "row"), None),
        P(("grp", "row")),
    )
    out_specs = (P(("grp", "row"), None), P(("grp", "row"), None), P(), P())
    return jax.shard_map(
        on_device, mesh=mesh, in_specs=in_specs, out_specs=out_specs, check_vma=False
    )
```

profile of v0, /device:TPU:8, one launch (start us, length us, event | category | flops | bytes accessed | tf_op | source)
XLA Modules:
  0.0 638.3 jit_solution(11707294678581093016)
XLA Ops:
  7.2 0.0 copy-start
  7.2 0.0 copy-start.1
  7.2 0.8 compare_select_fusion
  8.1 0.1 reshape.124
  8.2 3.6 gather_fusion.1
  11.7 5.5 all-to-all-start
  17.3 0.6 fusion.52
  22.9 0.8 broadcast_select_fusion
  23.7 0.0 all-reduce.10.cloned.1.call-update
  23.7 0.0 all-reduce.8.cloned.1.call-start
  23.8 0.6 eq.97
  24.4 0.6 slice_bitcast_fusion
  25.0 2.8 gather_fusion
  27.8 6.8 %fusion.25 = f32[64,256,128]{2,1,0:T(8,128)} fusion(bf16[64,128,256]{2,1,0:T(8,128)(2,1)} %gather_fusion, bf16[1,64,128,128]{3,2,1,0:T(8,128)(2,1)S(1)} %copy-done), kind=kOutput, calls=%fused_computation.44 | convolution fusion | flops 536870912 | bytes 14680064 | tf_op jit(solution)/shard_map/lab,lbf->laf/dot_general | solution.py:39
  34.6 9.2 %copy.25 = f32[64,256,128]{1,0,2:T(8,128)} copy(f32[64,256,128]{2,1,0:T(8,128)} %fusion.25) | data formatting | bytes 16777216 | tf_op jit(solution)/shard_map/lab,lbf->laf/dot_general | solution.py:39
  43.8 5.2 fusion.2
  48.9 2.6 copy.18
  51.5 2.9 copy.19
  54.4 0.7 convert_rsqrt_fusion
  55.2 1.8 fusion.53
  57.0 117.7 %all-reduce.10.cloned.1.call-done = (bf16[128,256]{1,0:T(8,128)(2,1)}, bf16[128,256]{1,0:T(8,128)(2,1)}, bf16[128,256]{1,0:T(8,128)(2,1)}, bf16[128,256]{1,0:T(8...) async-done(((bf16[128,256]{1,0:T(8,128)(2,1)}, bf16[128,256]{1,0:T(8,128)(2,1)}, ...) | async-done | bytes 524304 | tf_op jit(solution)/shard_map/psum | solution.py:12
  174.6 1.6 fusion.37
  176.2 0.0 copy-start.5
  176.2 1.6 convolution_add_fusion.8
  177.9 0.7 copy-done.5
  178.6 0.5 convolution_add_fusion.7
  179.1 0.4 copy-done.16
  179.4 0.5 convolution_add_fusion.6
  179.9 0.4 copy-done.15
  180.3 0.5 convolution_add_fusion.5
  180.7 0.4 copy-done.14
  181.1 0.5 convolution_add_fusion.4
  181.6 0.4 copy-done.13
  182.0 0.5 convolution_add_fusion.3
  182.4 1.1 copy-done.4
  183.5 1.8 fusion.9
  185.4 3.1 fusion.10
  188.5 3.0 fusion.15
  191.5 1.1 fusion.54
  192.7 1.2 convolution_bitcast_fusion.1
  193.9 2.7 fusion.12
  196.5 1.7 copy.29
  198.2 2.8 gather_fusion.2
  201.0 6.8 %fusion.23 = f32[64,256,128]{2,1,0:T(8,128)} fusion(bf16[64,128,256]{2,1,0:T(8,128)(2,1)} %gather_fusion.2, bf16[1,64,128,128]{3,2,1,0:T(8,128)(2,1)S(1)} %copy-done), kind=kOutput, calls=%fused_computation.42 | convolution fusion | flops 536870912 | bytes 14680064 | tf_op jit(solution)/shard_map/lab,laf->lbf/dot_general | solution.py:84
  207.8 9.2 %copy.27 = f32[64,256,128]{1,0,2:T(8,128)} copy(f32[64,256,128]{2,1,0:T(8,128)} %fusion.23) | data formatting | bytes 16777216 | tf_op jit(solution)/shard_map/lab,laf->lbf/dot_general | solution.py:84
  217.0 5.2 fusion
  222.2 2.6 copy.22
  224.8 0.0 all-reduce.8.cloned.1.call-update
  224.8 0.0 all-reduce.6.cloned.1.call-start
  224.8 3.4 fusion.28
  228.3 0.9 copy.30
  229.2 0.0 all-reduce.6.cloned.1.call-update
  229.2 2.7 fusion.29
  231.9 0.8 copy.23
  232.8 4.8 all-to-all-start.1
  237.6 3.4 convolution_add_fusion
  241.0 233.6 %all-reduce.8.cloned.1.call-done = (f32[256,256]{0,1:T(8,128)}, f32[256,256]{1,0:T(8,128)}) async-done(((f32[256,256]{0,1:T(8,128)}, f32[256,256]{1,0:T(8,128)}), (f32[256,256]{0,1:T(8,128)}, f32[256,256]{1,0:T(8,128)})) %all-reduce.8.cloned.1.call-update) | async-done | bytes 524304 | tf_op jit(solution)/shard_map/psum | solution.py:75
  474.6 1.8 copy.24
  476.4 148.1 %all-reduce.6.cloned.1.call-done = bf16[8,128,256]{1,0,2:T(8,128)(2,1)} async-done(((bf16[8,128,256]{1,0,2:T(8,128)(2,1)}), bf16[8,128,256]{1,0,2:T(8,128)(2,1)}) %all-reduce.6.cloned.1.call-update) | async-done | bytes 524304 | tf_op jit(solution)/shard_map/psum | solution.py:91
  624.6 1.3 fusion.46
  625.9 0.1 copy.28
  626.0 1.6 fusion.39
  627.6 3.4 fusion.11
  631.1 0.7 copy.43
  (46 shorter events, 0.1 us)
Async XLA Ops:
  7.2 20.6 %copy-start = (bf16[1,64,128,128]{3,2,1,0:T(8,128)(2,1)S(1)}, bf16[1,64,128,128]{3,2,1,0:T(8,128)(2,1)}, u32[]{:S(2)}) copy-start(bf16[1,64,128,128]{3,2,1,0:T(8,128)(2,1)} %param.17) | copy-start | bytes 6291460
  7.2 16.6 %copy-start.20 = (s32[1,8,64]{2,1,0:T(8,128)S(1)}, s32[1,8,64]{2,1,0:T(8,128)}, u32[]{:S(2)}) copy-start(s32[1,8,64]{2,1,0:T(8,128)} %param.21) | copy-start | bytes 6148
  7.2 15.7 %copy-start.1 = (bf16[2048,256]{1,0:T(8,128)(2,1)S(1)}, bf16[2048,256]{1,0:T(8,128)(2,1)}, u32[]{:S(2)}) copy-start(bf16[2048,256]{1,0:T(8,128)(2,1)} %param.13) | copy-start | bytes 3145732
  7.2 10.0 %copy-start.19 = (s32[1,8]{1,0:T(1,128)S(1)}, s32[1,8]{1,0:T(1,128)}, u32[]{:S(2)}) copy-start(s32[1,8]{1,0:T(1,128)} %param.20) | copy-start | bytes 100
  7.2 17.2 %copy-start.23 = (s32[1,64,2]{1,2,0:T(2,128)S(1)}, s32[1,64,2]{1,2,0:T(2,128)}, u32[]{:S(2)}) copy-start(s32[1,64,2]{1,2,0:T(2,128)} %param.18) | copy-start | bytes 1540
  11.7 173.6 %all-to-all-start = ((bf16[8,64,256]{2,1,0:T(8,128)(2,1)}), bf16[8,64,256]{2,1,0:T(8,128)(2,1)S(1)}, u32[]{:S(2)}, u32[]{:S(2)}) async-start(bf16[8,64,256]{2,1,0:T(8,128)(2,1)} %bitcast.18), calls=%async_computation | async-start | bytes 524288 | tf_op jit(solution)/shard_map/all_to_all | solution.py:53
  17.2 157.4 %all-reduce.10.cloned.1.call-start = ((), (), s32[]{:S(2)}) async-start(), calls=%async_computation.4 | async-start | bytes 1048576 | tf_op jit(solution)/shard_map/psum | solution.py:12
  23.7 450.9 %all-reduce.8.cloned.1.call-start = ((), (), s32[]{:S(2)}) async-start(), calls=%async_computation.3 | async-start | bytes 1048576 | tf_op jit(solution)/shard_map/psum | solution.py:75
  51.5 3.6 copy-start.8
  174.6 1.6 copy-start.18
  176.2 2.4 copy-start.5
  176.2 2.4 copy-start.17
  178.6 0.8 copy-start.16
  179.4 0.8 copy-start.15
  180.3 0.8 copy-start.14
  181.1 0.8 copy-start.13
  182.0 1.6 copy-start.4
  182.0 1.6 copy-start.12
  185.3 3.2 copy-start.7
  185.4 3.2 copy-start.10
  185.4 3.2 copy-start.24
  191.5 1.1 copy-start.2
  191.5 2.3 copy-start.11
  207.8 9.2 %copy-start.22 = (s32[64]{0:T(128)S(1)}, s32[64]{0:T(128)}, u32[]{:S(2)}) copy-start(s32[64]{0:T(128)} %get-tuple-element.44) | copy-start | bytes 772
  222.2 2.7 copy-start.6
  224.8 399.8 %all-reduce.6.cloned.1.call-start = ((), (), s32[]{:S(2)}) async-start(), calls=%async_computation.2 | async-start | bytes 1048576 | tf_op jit(solution)/shard_map/psum | solution.py:91
  229.2 8.4 %copy-start.3 = (bf16[2048,256]{1,0:T(8,128)(2,1)S(1)}, bf16[2048,256]{1,0:T(8,128)(2,1)}, u32[]{:S(2)}) copy-start(bf16[2048,256]{1,0:T(8,128)(2,1)} %copy-done.2) | copy-start | bytes 3145732
  232.8 394.9 %all-to-all-start.1 = ((bf16[8,64,256]{2,1,0:T(8,128)(2,1)}), bf16[8,64,256]{2,1,0:T(8,128)(2,1)S(1)}, u32[]{:S(2)}, u32[]{:S(2)}) async-start(bf16[8,64,256]{2,1,0:T(8,128)(2,1)} %bitcast.32), calls=%async_computation.1 | async-start | bytes 524288 | tf_op jit(solution)/shard_map/all_to_all | solution.py:99
  237.6 390.0 %copy-start.21 = (s32[512]{0:T(512)S(1)}, s32[512]{0:T(512)}, u32[]{:S(2)}) copy-start(s32[512]{0:T(512)} %eq.97) | copy-start | bytes 6148
  626.0 5.1 copy-start.9
Sparse Core Ops, SparseCore 0:
  23.8 150.7 all-reduce.9
  224.9 249.6 all-reduce.7
  478.4 146.1 all-reduce.5
where the time goes:
time: 640 us; the launch traced here: 638 us
  waiting for transfers between devices  499 us (78%)
  matrix products  58.4 us (9%)
  local copies, waits for them, and re-layouts  46.5 us (7%)
  between operations  19 us (3%)
  starting transfers between devices  10.4 us (2%)
    psum x1, waiting for transfers between devices, on_device(): lax.psum((self_part, neighbor_part), ('grp', 'row'))  234 us
    psum x1, waiting for transfers between devices, on_device(): totals = lax.psum(hub_terms.astype(jnp.bfloat16), 'row').astype(jnp.float32)  148 us
    psum x1, waiting for transfers between devices, spread(): return lax.psum(jnp.where(mine, value, jnp.zeros_like(value)), axis)  118 us
  transfers between devices with their start and end apart: 5, of which 3 were waited for; matrix products, arithmetic and copies ran while one was open for 9% of the time, Pallas kernels for 0%

commit v1 on v0

--- a/solution.py
+++ b/solution.py
@@ -72,7 +72,8 @@
     neighbor_part = lax.dot_general(
         aggregated, grad_before, rows_dims, preferred_element_type=jnp.float32
     )
-    grad_self, grad_neighbor = lax.psum((self_part, neighbor_part), ("grp", "row"))
+    launch_the_array = lambda local_array: jax.lax.psum(jax.lax.psum(local_array, "row"), "grp")
+    grad_self, grad_neighbor = launch_the_array((self_part, neighbor_part))
     grad_aggregate = (
         lax.dot_general(grad_before, neighbor_weight, cols_dims, preferred_element_type=jnp.float32)
         * scaling

time: 640 us -> 600 us (0.938)
  waiting for transfers between devices: 499 us -> 454 us
    psum x1 -> x2, waiting for transfers between devices: 234 us -> 205 us  [the longest x1 147 us: on_device(): jax.lax.psum(local_array, 'row')]
    psum x1, waiting for transfers between devices: 148 us -> 131 us  [on_device(): totals = lax.psum(hub_terms.astype(jnp.bfloat16), 'row').astype(jnp.float32)]
  transfers between devices with their start and end apart: 5 -> 6, of which waited for: 3 -> 4; matrix products, arithmetic and copies ran while one was open for 9% -> 10% of each run, Pallas kernels for 0% -> 0%
where the time goes in v1:
time: 600 us; the launch traced here: 597 us
  waiting for transfers between devices  454 us (76%)
  matrix products  58.4 us (10%)
  local copies, waits for them, and re-layouts  50.2 us (8%)
  between operations  19.1 us (3%)
  starting transfers between devices  10.4 us (2%)
    psum x1, waiting for transfers between devices, on_device(): jax.lax.psum(local_array, 'row')  147 us
    psum x1, waiting for transfers between devices, on_device(): totals = lax.psum(hub_terms.astype(jnp.bfloat16), 'row').astype(jnp.float32)  131 us
    psum x1, waiting for transfers between devices, spread(): return lax.psum(jnp.where(mine, value, jnp.zeros_like(value)), axis)  118 us
    psum x1, waiting for transfers between devices, on_device(): jax.lax.psum(jax.lax.psum(local_array, 'row'), 'grp')  58.2 us
  transfers between devices with their start and end apart: 6, of which 4 were waited for; matrix products, arithmetic and copies ran while one was open for 10% of the time, Pallas kernels for 0%

profile of v1, /device:TPU:8, one launch (start us, length us, event | category | flops | bytes accessed | tf_op | source)
XLA Modules:
  0.0 597.0 jit_solution(7922504569740643192)
XLA Ops:
  7.2 0.8 compare_select_fusion
  8.1 0.1 reshape.124
  8.2 3.6 gather_fusion.1
  11.7 5.5 all-to-all-start
  17.3 0.6 fusion.52
  23.0 0.8 broadcast_select_fusion
  23.8 0.0 all-reduce.14.cloned.1.call-update
  23.8 0.0 all-reduce.8.cloned.1.call-start
  23.8 0.7 eq.97
  24.5 0.6 slice_bitcast_fusion
  25.1 2.8 gather_fusion
  27.9 6.8 %fusion.25 = f32[64,256,128]{2,1,0:T(8,128)} fusion(bf16[64,128,256]{2,1,0:T(8,128)(2,1)} %gather_fusion, bf16[1,64,128,128]{3,2,1,0:T(8,128)(2,1)S(1)} %copy-done), kind=kOutput, calls=%fused_computation.44 | convolution fusion | flops 536870912 | bytes 14680064 | tf_op jit(solution)/shard_map/lab,lbf->laf/dot_general | solution.py:39
  34.7 9.2 %copy.25 = f32[64,256,128]{1,0,2:T(8,128)} copy(f32[64,256,128]{2,1,0:T(8,128)} %fusion.25) | data formatting | bytes 16777216 | tf_op jit(solution)/shard_map/lab,lbf->laf/dot_general | solution.py:39
  43.9 5.2 fusion.2
  49.0 2.6 copy.18
  51.6 2.9 copy.19
  54.6 0.7 convert_rsqrt_fusion
  55.3 1.8 fusion.53
  57.1 117.7 %all-reduce.14.cloned.1.call-done = (bf16[128,256]{1,0:T(8,128)(2,1)}, bf16[128,256]{1,0:T(8,128)(2,1)}, bf16[128,256]{1,0:T(8,128)(2,1)}, bf16[128,256]{1,0:T(8...) async-done(((bf16[128,256]{1,0:T(8,128)(2,1)}, bf16[128,256]{1,0:T(8,128)(2,1)}, ...) | async-done | bytes 524304 | tf_op jit(solution)/shard_map/psum | solution.py:12
  174.7 1.6 fusion.37
  176.3 1.6 convolution_add_fusion.8
  178.0 0.7 copy-done.5
  178.7 0.5 convolution_add_fusion.7
  179.2 0.4 copy-done.17
  179.5 0.5 convolution_add_fusion.6
  180.0 0.4 copy-done.16
  180.4 0.5 convolution_add_fusion.5
  180.8 0.4 copy-done.15
  181.2 0.5 convolution_add_fusion.4
  181.7 0.4 copy-done.14
  182.0 0.5 convolution_add_fusion.3
  182.5 1.1 copy-done.4
  183.6 1.8 fusion.9
  185.5 3.1 fusion.10
  188.7 3.0 fusion.15
  191.7 1.0 copy-done.2
  192.6 1.4 fusion.12
  194.1 2.3 copy.29
  196.4 4.7 fusion.28
  201.1 0.7 fusion.29
  201.8 4.1 gather_fusion.2
  205.8 6.8 %fusion.23 = f32[64,256,128]{2,1,0:T(8,128)} fusion(bf16[64,128,256]{2,1,0:T(8,128)(2,1)} %gather_fusion.2, bf16[1,64,128,128]{3,2,1,0:T(8,128)(2,1)S(1)} %copy-done), kind=kOutput, calls=%fused_computation.42 | convolution fusion | flops 536870912 | bytes 14680064 | tf_op jit(solution)/shard_map/lab,laf->lbf/dot_general | solution.py:85
  212.6 9.2 %copy.27 = f32[64,256,128]{1,0,2:T(8,128)} copy(f32[64,256,128]{2,1,0:T(8,128)} %fusion.23) | data formatting | bytes 16777216 | tf_op jit(solution)/shard_map/lab,laf->lbf/dot_general | solution.py:85
  221.8 5.2 fusion
  227.0 2.6 copy.22
  229.6 0.9 copy.30
  230.5 0.0 all-reduce.8.cloned.1.call-update
  230.5 0.8 copy.23
  231.3 4.8 all-to-all-start.1
  236.1 2.8 fusion.54
  238.9 1.2 convolution_bitcast_fusion.1
  240.1 0.0 all-reduce.10.cloned.1.call-update
  240.1 0.0 all-reduce.12.cloned.1.call-start
  240.2 3.7 convolution_add_fusion
  243.9 131.4 %all-reduce.8.cloned.1.call-done = bf16[8,128,256]{1,0,2:T(8,128)(2,1)} async-done(((bf16[8,128,256]{1,0,2:T(8,128)(2,1)}), bf16[8,128,256]{1,0,2:T(8,128)(2,1)}) %all-reduce.8.cloned.1.call-update) | async-done | bytes 524304 | tf_op jit(solution)/shard_map/psum | solution.py:92
  375.3 1.3 fusion.46
  376.6 0.1 copy.28
  376.7 147.1 %all-reduce.10.cloned.1.call-done = (f32[256,256]{0,1:T(8,128)}, f32[256,256]{1,0:T(8,128)}) async-done(((f32[256,256]{0,1:T(8,128)}, f32[256,256]{1,0:T(8,128)}), (f32[256,256]{0,1:T(8,128)}, f32[256,256]{1,0:T(8,128)})) %all-reduce.10.cloned.1.call-update) | async-done | bytes 524304 | tf_op jit(solution)/shard_map/psum | solution.py:75
  523.8 0.0 all-reduce.12.cloned.1.call-update
  523.8 1.6 fusion.39
  525.4 3.4 fusion.11
  528.8 58.2 %all-reduce.12.cloned.1.call-done = (f32[256,256]{0,1:T(8,128)}, f32[256,256]{1,0:T(8,128)}) async-done(((f32[256,256]{0,1:T(8,128)}, f32[256,256]{1,0:T(8,128)}), (f32[256,256]{0,1:T(8,128)}, f32[256,256]{1,0:T(8,128)})) %all-reduce.12.cloned.1.call-update) | async-done | bytes 524304 | tf_op jit(solution)/shard_map/psum | solution.py:75
  587.0 1.8 copy.24
  588.8 1.7 copy.45
  (51 shorter events, 0.1 us)
Async XLA Ops:
  7.2 20.7 %copy-start = (bf16[1,64,128,128]{3,2,1,0:T(8,128)(2,1)S(1)}, bf16[1,64,128,128]{3,2,1,0:T(8,128)(2,1)}, u32[]{:S(2)}) copy-start(bf16[1,64,128,128]{3,2,1,0:T(8,128)(2,1)} %param.17) | copy-start | bytes 6291460
  7.2 16.7 %copy-start.21 = (s32[1,8,64]{2,1,0:T(8,128)S(1)}, s32[1,8,64]{2,1,0:T(8,128)}, u32[]{:S(2)}) copy-start(s32[1,8,64]{2,1,0:T(8,128)} %param.21) | copy-start | bytes 6148
  7.2 15.8 %copy-start.1 = (bf16[2048,256]{1,0:T(8,128)(2,1)S(1)}, bf16[2048,256]{1,0:T(8,128)(2,1)}, u32[]{:S(2)}) copy-start(bf16[2048,256]{1,0:T(8,128)(2,1)} %param.13) | copy-start | bytes 3145732
  7.2 10.0 %copy-start.20 = (s32[1,8]{1,0:T(1,128)S(1)}, s32[1,8]{1,0:T(1,128)}, u32[]{:S(2)}) copy-start(s32[1,8]{1,0:T(1,128)} %param.20) | copy-start | bytes 100
  7.2 17.3 %copy-start.24 = (s32[1,64,2]{1,2,0:T(2,128)S(1)}, s32[1,64,2]{1,2,0:T(2,128)}, u32[]{:S(2)}) copy-start(s32[1,64,2]{1,2,0:T(2,128)} %param.18) | copy-start | bytes 1540
  11.7 173.7 %all-to-all-start = ((bf16[8,64,256]{2,1,0:T(8,128)(2,1)}), bf16[8,64,256]{2,1,0:T(8,128)(2,1)S(1)}, u32[]{:S(2)}, u32[]{:S(2)}) async-start(bf16[8,64,256]{2,1,0:T(8,128)(2,1)} %bitcast.18), calls=%async_computation | async-start | bytes 524288 | tf_op jit(solution)/shard_map/all_to_all | solution.py:53
  17.2 157.5 %all-reduce.14.cloned.1.call-start = ((), (), s32[]{:S(2)}) async-start(), calls=%async_computation.5 | async-start | bytes 1048576 | tf_op jit(solution)/shard_map/psum | solution.py:12
  23.8 351.5 %all-reduce.8.cloned.1.call-start = ((), (), s32[]{:S(2)}) async-start(), calls=%async_computation.2 | async-start | bytes 1048576 | tf_op jit(solution)/shard_map/psum | solution.py:92
  51.6 3.7 copy-start.11
  174.7 1.6 copy-start.19
  176.3 2.4 copy-start.5
  176.3 2.4 copy-start.18
  178.7 0.8 copy-start.17
  179.5 0.8 copy-start.16
  180.4 0.8 copy-start.15
  181.2 0.8 copy-start.14
  182.0 1.6 copy-start.4
  182.0 1.6 copy-start.13
  185.5 3.2 copy-start.9
  185.5 3.2 copy-start.12
  185.5 3.2 copy-start.25
  188.6 3.0 copy-start.7
  191.7 1.0 copy-start.2
  196.4 4.7 copy-start.6
  196.4 4.7 copy-start.8
  212.6 9.2 %copy-start.23 = (s32[64]{0:T(128)S(1)}, s32[64]{0:T(128)}, u32[]{:S(2)}) copy-start(s32[64]{0:T(128)} %get-tuple-element.46) | copy-start | bytes 772
  227.0 2.6 copy-start.10
  231.3 294.1 %all-to-all-start.1 = ((bf16[8,64,256]{2,1,0:T(8,128)(2,1)}), bf16[8,64,256]{2,1,0:T(8,128)(2,1)S(1)}, u32[]{:S(2)}, u32[]{:S(2)}) async-start(bf16[8,64,256]{2,1,0:T(8,128)(2,1)} %bitcast.32), calls=%async_computation.1 | async-start | bytes 524288 | tf_op jit(solution)/shard_map/all_to_all | solution.py:100
  236.1 287.7 %all-reduce.10.cloned.1.call-start = ((), (), s32[]{:S(2)}) async-start(), calls=%async_computation.3 | async-start | bytes 1048576 | tf_op jit(solution)/shard_map/psum | solution.py:75
  236.1 2.8 copy-start.3
  240.1 346.9 %all-reduce.12.cloned.1.call-start = ((), (), s32[]{:S(2)}) async-start(), calls=%async_computation.4 | async-start | bytes 1048576 | tf_op jit(solution)/shard_map/psum | solution.py:75
  240.2 285.2 %copy-start.22 = (s32[512]{0:T(512)S(1)}, s32[512]{0:T(512)}, u32[]{:S(2)}) copy-start(s32[512]{0:T(512)} %eq.97) | copy-start | bytes 6148
Sparse Core Ops, SparseCore 0:
  23.9 150.7 all-reduce.13
  230.6 144.6 all-reduce.7
  379.3 144.4 all-reduce.9
  526.2 60.7 all-reduce.11
